TPU v7x, 32 devices: a whole 2x2x4 slice. The times are simulated.
32 devices in a mesh: shot: 8 (over z, x), rcv: 4 (over y, core).
Axes of the slice: x: 2, y: 2, z: 4, core: 2. Of those that a mesh axis runs over, the one named last changes fastest.
Arguments:
- traces: bfloat16 [256, 256, 1024], P('shot', 'rcv'), may hold values from -6 to 6
- aperture_lists: int32 [8, 4, 8], P('shot', 'rcv'), may hold values from 0 to 7, as said below
- aperture_counts: int32 [8, 4], P('shot', 'rcv'), may hold values from 4 to 8
Outputs:
- multiples: float32 [64, 2, 256, 256], P(None, None, 'shot', 'rcv')
Inputs may be any that keep to these rules, and one draw needn't show every extreme that they name: `aperture_lists`: for tile (i, j), entries 0 to aperture_counts[i, j] - 1 are consecutive rising x-block numbers (block b covers positions b * 32 to (b + 1) * 32 - 1) near the midpoint of the tile's shots and receivers; the other entries are 0.
All inputs are finite; a program needn't handle non-finite values.
Results may differ from a plain program's by a relative error of at most 0.0052.
Values may be sent and summed in bfloat16 or wider, within the bound.
No kernel may reach another device: no remote copies, remote signals or barrier semaphores. Data moves between devices by JAX's collectives and lax.ppermute only.
A program may use at most 128 MiB of HBM per device.

v0:
```python
import math

import jax
import jax.numpy as jnp
from jax import lax
from jax.sharding import PartitionSpec as P

SHOTS_PER_INDEX = 32
NT = 1024
BAND = 32
APB = 8
FIRST = 32
SECOND = 128
FREQS = 64


def dft_table():
    sample = jnp.arange(NT, dtype=jnp.int32)
    freq_bins = jnp.concatenate(
        [FIRST + jnp.arange(BAND, dtype=jnp.int32), SECOND + jnp.arange(BAND, dtype=jnp.int32)]
    )
    phase = (sample[:, None] * freq_bins[None, :] % NT).astype(jnp.float32) * (2.0 * math.pi / NT)
    factor = 1.0 / math.sqrt(NT)
    return (jnp.concatenate([jnp.cos(phase), -jnp.sin(phase)], axis=1) * factor).astype(
        jnp.bfloat16
    )


def spectra(traces):
    shots, receivers, samples = traces.shape
    flat = jnp.dot(
        traces.reshape(shots * receivers, samples), dft_table(), preferred_element_type=jnp.float32
    )
    flat = flat.astype(jnp.bfloat16)
    return flat.reshape(shots, receivers, 2, FREQS).transpose(3, 2, 0, 1)


def complex_product(left, right):

    def mult(leading_operand, trailing_operand):
        return jnp.einsum(
            "ylp,ypi->yli", leading_operand, trailing_operand, preferred_element_type=jnp.float32
        )

    real_out = mult(left[:, 0], right[:, 0]) - mult(left[:, 1], right[:, 1])
    imag_out = mult(left[:, 0], right[:, 1]) + mult(left[:, 1], right[:, 0])
    return jnp.stack([real_out, imag_out], axis=1)


def local(traces, aperture_lists, aperture_counts):
    trace_spectrum = spectra(traces)
    slots = jnp.arange(APB, dtype=jnp.int32)
    shot_rows = lax.all_gather(trace_spectrum, "rcv", axis=3, tiled=True)
    column_list, column_count = (
        lax.all_gather(aperture_lists, "shot", axis=0, tiled=True),
        lax.all_gather(aperture_counts, "shot", axis=0, tiled=True),
    )
    own_block = lax.axis_index("shot")
    column_live = slots[None, :] < column_count[:, 0][:, None]
    named = jnp.any(column_live & (column_list[:, 0, :] == own_block), axis=1).astype(jnp.bfloat16)
    owners = named.shape[0]
    outgoing = trace_spectrum[:, :, None, :, :] * named[None, None, :, None, None]
    outgoing = outgoing.reshape(
        trace_spectrum.shape[0], 2, owners * trace_spectrum.shape[2], trace_spectrum.shape[3]
    )
    received_block = lax.all_to_all(outgoing, "shot", split_axis=2, concat_axis=2, tiled=True)
    total = complex_product(shot_rows, received_block)
    return total * (1.0 / math.sqrt(APB * SHOTS_PER_INDEX))


def solution(mesh):
    placed = (P("shot", "rcv", None), P("shot", "rcv", None), P("shot", "rcv"))
    return jax.shard_map(
        local, mesh=mesh, in_specs=placed, out_specs=P(None, None, "shot", "rcv"), check_vma=False
    )
```

profile of v0, /device:TPU:0, one launch (start us, length us, event | category | flops | bytes accessed | tf_op | source)
XLA Modules:
  0.0 208.7 jit_solution(15441817494235408101)
XLA Ops:
  6.5 0.1 pad_add_fusion
  6.6 2.1 fusion.34
  9.4 1.2 dynamic-slice
  10.6 4.0 %fusion = bf16[2048,128]{0,1:T(8,128)(2,1)S(1)} fusion(bf16[2048,1024]{1,0:T(8,128)(2,1)} %bitcast.57, f32[1024,64]{1,0:T(8,128)S(1)} %get-tuple-element.10, f32[1024,64]{1,0:T(8,128)S(1)} %get-tuple-element.9), kind=kOutput, calls=%fused_computation.2 | convolution fusion | flops 537526272 | bytes 5242880 | tf_op jit(solution)/shard_map/dot_general | solution.py:31
  14.6 0.7 bitcast_dynamic-update-slice_fusion
  15.3 1.1 reshape.17
  16.3 13.1 %all-reduce = s32[8]{0:T(128)S(1)} all-reduce(s32[8]{0:T(128)S(1)} %bitcast_dynamic-update-slice_fusion), channel_id=1, replica_groups=mesh['shot'=8,'rcv'=4] {'shot'}, use_global_device_ids=true, to_apply=%add | all-reduce | flops 8 | bytes 64
  29.5 17.9 %all_gather.11 = s32[8,1,8]{2,1,0:T(1,128)S(1)} all-gather(s32[1,1,8]{2,1,0:T(1,128)S(1)} %copy-done.2), channel_id=1, replica_groups=mesh['shot'=8,'rcv'=4] {'shot'}, dimensions={0}, use_global_device_ids=true | all-gather | bytes 288 | tf_op jit(solution)/shard_map/all_gather | solution.py:55
  47.4 0.2 fusion.36
  47.6 0.1 mul.60
  47.7 0.1 mul.61
  47.7 6.0 %bitcast_multiply_fusion = bf16[64,2,256,64]{3,2,1,0:T(8,128)(2,1)} fusion(bf16[256]{0:T(256)(128)(2,1)S(1)} %mul.61, bf16[32,64,2,64]{1,0,3,2:T(8,128)(2,1)S(1)} %reshape.17), kind=kLoop, calls=%fused_computation | loop fusion | flops 8388608 | bytes 4719104 | tf_op jit(solution)/shard_map/mul | solution.py:62
  53.7 12.0 %copy.28 = bf16[64,2,256,64]{3,0,1,2:T(8,128)(2,1)} copy(bf16[64,2,256,64]{3,2,1,0:T(8,128)(2,1)} %bitcast_multiply_fusion) | data formatting | bytes 8388608 | tf_op jit(solution)/shard_map/mul | solution.py:62
  65.7 10.5 %reshape.24 = bf16[8,2,131072]{2,1,0:T(2,128)(2,1)} reshape(bf16[256,2,64,64]{3,2,1,0:T(8,128)(2,1)} %bitcast.56) | data formatting | bytes 8388608
  76.2 4.6 %all-to-all-start = ((bf16[8,2,131072]{2,1,0:T(2,128)(2,1)}), bf16[8,2,131072]{2,1,0:T(2,128)(2,1)}, u32[]{:S(2)}, u32[]{:S(2)}) async-start(bf16[8,2,131072]{2,1,0:T(2,128)(2,1)} %reshape.24), calls=%async_computation | async-start | bytes 8388608 | tf_op jit(solution)/shard_map/all_to_all | solution.py:66
  80.8 0.3 all-gather.2.cloned.1.call-start
  81.1 2.9 %copy.11 = bf16[32,64,2,64]{3,0,2,1:T(8,128)(2,1)} copy(bf16[32,64,2,64]{1,0,3,2:T(8,128)(2,1)S(1)} %reshape.17) | data formatting | bytes 1048576 | tf_op jit(solution)/shard_map/reshape | solution.py:35
  84.0 35.7 %all-gather.2.cloned.1.call-done = bf16[64,2,32,256]{0,2,1,3:T(8,128)(2,1)} async-done(((bf16[64,2,32,64]{0,2,1,3:T(8,128)(2,1)}), bf16[64,2,32,256]{0,2,1,3:T(8,128)(2,1)}) %all-gather.2.cloned.1.call-update) | async-done | bytes 2097168 | tf_op jit(solution)/shard_map/all_gather | solution.py:53
  119.7 4.3 %fusion.40 = (bf16[64,1,32,256]{0,2,1,3:T(8,128)(2,1)}, bf16[64,1,32,256]{0,2,1,3:T(8,128)(2,1)S(1)}) fusion(bf16[64,2,32,256]{0,2,1,3:T(8,128)(2,1)} %all-gather.2.cloned.1.call-done), kind=kLoop, calls=%fused_computation.44 | loop fusion | bytes 4194304 | tf_op jit(solution)/shard_map/slice | solution.py:45
  124.0 4.1 %copy.23 = bf16[64,1,32,256]{3,2,0,1:T(8,128)(2,1)S(1)} copy(bf16[64,1,32,256]{0,2,1,3:T(8,128)(2,1)} %get-tuple-element.7) | data formatting | bytes 2097152
  128.1 3.6 %copy.21 = bf16[64,1,32,256]{3,2,0,1:T(8,128)(2,1)} copy(bf16[64,1,32,256]{0,2,1,3:T(8,128)(2,1)S(1)} %get-tuple-element.8) | data formatting | bytes 2097152
  131.7 36.1 %all-to-all-done = bf16[8,2,131072]{2,1,0:T(2,128)(2,1)} async-done(((bf16[8,2,131072]{2,1,0:T(2,128)(2,1)}), bf16[8,2,131072]{2,1,0:T(2,128)(2,1)}, u32[]{:S(2)}, u32[]{:S(2)}) %all-to-all-start) | async-done | bytes 4194336 | tf_op jit(solution)/shard_map/all_to_all | solution.py:66
  167.8 10.3 %reshape.25 = bf16[256,2,64,64]{3,2,1,0:T(8,128)(2,1)} reshape(bf16[8,2,131072]{2,1,0:T(2,128)(2,1)} %all-to-all-done) | data formatting | bytes 8388608
  178.1 6.5 %fusion.39 = (bf16[64,1,256,64]{3,0,1,2:T(8,128)(2,1)}, bf16[64,1,256,64]{3,0,1,2:T(8,128)(2,1)}) fusion(bf16[64,2,256,64]{3,0,1,2:T(8,128)(2,1)} %bitcast.55), kind=kLoop, calls=%fused_computation.43 | loop fusion | bytes 8388608 | tf_op jit(solution)/shard_map/slice | solution.py:45
  184.6 5.9 %copy.24 = bf16[64,1,256,64]{2,3,0,1:T(8,128)(2,1)} copy(bf16[64,1,256,64]{3,0,1,2:T(8,128)(2,1)} %get-tuple-element.6) | data formatting | bytes 4194304
  190.5 4.9 %copy.22 = bf16[64,1,256,64]{2,3,0,1:T(8,128)(2,1)S(1)} copy(bf16[64,1,256,64]{3,0,1,2:T(8,128)(2,1)} %get-tuple-element.5) | data formatting | bytes 4194304
  195.4 2.4 %fusion.3 = f32[64,32,64]{2,1,0:T(8,128)S(1)} fusion(bf16[64,1,256,64]{2,3,0,1:T(8,128)(2,1)} %copy.24, bf16[64,1,32,256]{3,2,0,1:T(8,128)(2,1)S(1)} %copy.23), kind=kOutput, calls=%fused_computation.6 | convolution fusion | flops 67108864 | bytes 3670016 | tf_op jit(solution)/shard_map/ylp,ypi->yli/dot_general | solution.py:41
  197.9 0.7 fusion.1
  198.6 0.7 fusion.12
  199.3 0.7 fusion.18
  200.0 0.3 maximum_multiply_fusion
  200.3 1.5 copy.19
  (10 shorter events, 0.1 us)
Async XLA Ops:
  10.6 18.9 %copy-start.2 = (s32[1,1,8]{2,1,0:T(1,128)S(1)}, s32[1,1,8]{2,1,0:T(1,128)}, u32[]{:S(2)}) copy-start(s32[1,1,8]{2,1,0:T(1,128)} %param.4) | copy-start | bytes 100
  76.2 91.6 %all-to-all-start = ((bf16[8,2,131072]{2,1,0:T(2,128)(2,1)}), bf16[8,2,131072]{2,1,0:T(2,128)(2,1)}, u32[]{:S(2)}, u32[]{:S(2)}) async-start(bf16[8,2,131072]{2,1,0:T(2,128)(2,1)} %reshape.24), calls=%async_computation | async-start | bytes 8388608 | tf_op jit(solution)/shard_map/all_to_all | solution.py:66
  80.8 38.9 %all-gather.2.cloned.1.call-start = ((), (), s32[]{:S(2)}) async-start(), calls=%async_computation.1 | async-start | bytes 5242880 | tf_op jit(solution)/shard_map/all_gather | solution.py:53
  195.4 2.4 %copy-start = (bf16[64,1,256,64]{2,3,0,1:T(8,128)(2,1)S(1)}, bf16[64,1,256,64]{2,3,0,1:T(8,128)(2,1)}, u32[]{:S(2)}) copy-start(bf16[64,1,256,64]{2,3,0,1:T(8,128)(2,1)} %copy.24) | copy-start | bytes 6291460
  195.4 2.5 %copy-start.1 = (bf16[64,1,32,256]{3,2,0,1:T(8,128)(2,1)S(1)}, bf16[64,1,32,256]{3,2,0,1:T(8,128)(2,1)}, u32[]{:S(2)}) copy-start(bf16[64,1,32,256]{3,2,0,1:T(8,128)(2,1)} %copy.21) | copy-start | bytes 3145732
Sparse Core Ops, SparseCore 0:
  84.1 35.5 all-gather.1
where the time goes:
time: 210 us; the launch traced here: 209 us
  waiting for transfers between devices  71.8 us (34%)
  local copies, waits for them, and re-layouts  69.7 us (33%)
  blocking collectives  31 us (15%)
  between operations  14.2 us (7%)
  other arithmetic  8.59 us (4%)
  matrix products  8.46 us (4%)
  starting transfers between devices  4.85 us (2%)
    unnamed x15, local copies, waits for them, and re-layouts  41.3 us
    all_to_all x1, waiting for transfers between devices, local(): lax.all_to_all(outgoing, 'shot', split_axis=2, concat_axis=2, tiled=True)  36.1 us
    all_gather x1, waiting for transfers between devices, local(): shot_rows = lax.all_gather(trace_spectrum, 'rcv', axis=3, tiled=True)  35.7 us
    all_gather x1, blocking collectives, local(): lax.all_gather(aperture_lists, 'shot', axis=0, tiled=True)  17.9 us
    unnamed x1, blocking collectives  13.1 us
    mul x3, local copies, waits for them, and re-layouts, local(): trace_spectrum[:, :, None, :, :] * named[None, None, :, None, None]  12.2 us
    slice x2, local copies, waits for them, and re-layouts, complex_product(): real_out = mult(left[:, 0], right[:, 0]) - mult(left[:, 1], right[:, 1])  10.8 us
    mul x1, other arithmetic, local(): trace_spectrum[:, :, None, :, :] * named[None, None, :, None, None]  5.97 us
  transfers between devices with their start and end apart: 2, of which 2 were waited for; matrix products, arithmetic and copies ran while one was open for 7% of the time, Pallas kernels for 0%

commit v1 on v0

v1 whole, which is shorter than its diff:
```python
import functools
import math

import jax
import jax.numpy as jnp
import numpy as np
from jax import lax
from jax.experimental import pallas as pl
from jax.experimental.pallas import tpu as pltpu
from jax.sharding import PartitionSpec as P

BAND = 32
FIRST = 32
SECOND = 128
FREQS = 64
APB = 8
LANES = 128


def dft_rows(samples):
    bins = np.concatenate([FIRST + np.arange(BAND), SECOND + np.arange(BAND)])
    phase = (bins[:, None] * np.arange(samples)[None, :] % samples) * (2.0 * math.pi / samples)
    rows = np.stack([np.cos(phase), -np.sin(phase)], axis=1) / math.sqrt(samples)
    return rows.reshape(2 * FREQS, samples).astype(jnp.bfloat16)


def spectra_kernel(mask_rows, list_ref, count_ref, traces_ref, table_ref, out_ref, held):
    step, steps = pl.program_id(0), pl.num_programs(0)
    group, receivers = traces_ref.shape[1], traces_ref.shape[2]
    destinations = out_ref.shape[0]
    half = group * steps
    for a in range(group):
        pair = jnp.concatenate([traces_ref[0, a], traces_ref[1, a]], axis=0)
        held[pl.ds((step * group + a) * LANES, LANES), :] = lax.dot_general(
            table_ref[...], pair, (((1,), (1,)), ((), ())), preferred_element_type=jnp.float32
        )

    @pl.when(step == steps - 1)
    def _():
        low = lax.broadcasted_iota(jnp.int32, (half, LANES), 1) < receivers
        per = FREQS // destinations
        for q in range(FREQS):
            real = held[pl.ds(2 * q, half, stride=LANES), :]
            imag = held[pl.ds(2 * q + 1, half, stride=LANES), :]
            first = jnp.where(low, real, pltpu.roll(imag, receivers, 1))
            second = jnp.where(low, pltpu.roll(real, receivers, 1), imag)
            base = (q % per) * 2 * half
            out_ref[q // per, base : base + half, :] = first.astype(jnp.bfloat16)
            out_ref[q // per, base + half : base + 2 * half, :] = second.astype(jnp.bfloat16)
        parts = receivers // (2 * half)
        lane = lax.broadcasted_iota(jnp.int32, (mask_rows, LANES), 1)
        block = lax.broadcasted_iota(jnp.int32, (mask_rows, LANES), 0) * parts + lane % receivers // (2 * half)
        member = jnp.zeros((mask_rows, LANES), jnp.float32)
        for slot in range(APB):
            live = jnp.logical_and(block == list_ref[0, 0, slot], slot < count_ref[0, 0])
            member = jnp.where(live, 1.0, member)
        member = member.astype(jnp.bfloat16)
        for d in range(destinations):
            out_ref[d, per * 2 * half :, :] = member


def spectra(traces, aperture_lists, aperture_counts, destinations, mask_rows):
    shots, receivers, samples = traces.shape
    half = shots // 2
    group = 4
    rows = FREQS // destinations * shots + mask_rows
    return pl.pallas_call(
        functools.partial(spectra_kernel, mask_rows),
        grid=(half // group,),
        in_specs=[
            pl.BlockSpec(memory_space=pltpu.SMEM),
            pl.BlockSpec(memory_space=pltpu.SMEM),
            pl.BlockSpec((2, group, receivers, samples), lambda g: (0, g, 0, 0)),
            pl.BlockSpec((2 * FREQS, samples), lambda g: (0, 0)),
        ],
        out_specs=pl.BlockSpec((destinations, rows, LANES), lambda g: (0, 0, 0)),
        out_shape=jax.ShapeDtypeStruct((destinations, rows, LANES), jnp.bfloat16),
        scratch_shapes=[pltpu.VMEM((half * LANES, LANES), jnp.float32)],
        name="spectra",
    )(
        aperture_lists,
        aperture_counts,
        traces.reshape(2, half, receivers, samples),
        jnp.asarray(dft_rows(samples)),
    )


def products_kernel(tile_rows, tile_columns, own, shots, scale, *refs):
    if own:
        left_ref, right_ref, out_ref, left, right = refs
        columns, right_of = (0,), lambda i, j: i
        left_of = lambda i, j: j * tile_rows + i
        out_of = lambda i, j: i
    else:
        left_ref, out_ref, left, right = refs
        right_ref = left_ref
        columns = range(tile_columns)
        left_of = right_of = out_of = lambda i, j: i * tile_columns + j
    receivers = LANES // 2
    parts = receivers // shots
    freqs = out_ref.shape[1] // shots
    sign = jnp.where(lax.broadcasted_iota(jnp.int32, (shots, LANES), 1) < receivers, -1.0, 1.0)
    for q in range(freqs):
        rows = slice(q * shots, (q + 1) * shots)
        for j in columns:
            for b in range(tile_rows):
                block = right_ref[right_of(b, j), rows, :]
                turned = pltpu.roll(block.astype(jnp.float32), receivers, 1) * sign
                base = b // parts * LANES + b % parts * shots
                right[j, base : base + shots, :] = block
                right[j, base + receivers : base + receivers + shots, :] = turned.astype(jnp.bfloat16)
            for i in range(tile_rows):
                for k in range(tile_columns):
                    m = freqs * shots + k
                    member = right_ref[right_of(i, j), m : m + 1, :]
                    left[j, i * shots : (i + 1) * shots, k * LANES : (k + 1) * LANES] = left_ref[left_of(i, k), rows, :] * member
            total = jnp.dot(left[j], right[j], preferred_element_type=jnp.float32) * scale
            total = total.astype(jnp.bfloat16)
            for i in range(tile_rows):
                out_ref[out_of(i, j), rows, :] = total[i * shots : (i + 1) * shots, :]


def products(left, right, tile_rows, tile_columns, shots, freqs):
    own = right is not None
    operands = (left, right) if own else (left,)
    columns = 1 if own else tile_columns
    return pl.pallas_call(
        functools.partial(
            products_kernel, tile_rows, tile_columns, own, shots, 1.0 / math.sqrt(APB * shots)
        ),
        out_shape=jax.ShapeDtypeStruct((tile_rows * columns, freqs * shots, LANES), jnp.bfloat16),
        in_specs=[pl.BlockSpec(memory_space=pltpu.VMEM)] * len(operands),
        out_specs=pl.BlockSpec(memory_space=pltpu.VMEM),
        scratch_shapes=[
            pltpu.VMEM((columns, tile_rows * shots, tile_columns * LANES), jnp.bfloat16),
            pltpu.VMEM((columns, tile_columns * LANES, LANES), jnp.bfloat16),
        ],
        name="products",
    )(*operands)


def output_kernel(in_ref, out_ref):
    receivers = out_ref.shape[3]
    block = in_ref[...].astype(jnp.float32)
    out_ref[:, 0] = block[:, :, :receivers]
    out_ref[:, 1] = block[:, :, receivers:]


def output(arrived):
    freqs, shots, lanes = arrived.shape
    step = 16
    return pl.pallas_call(
        output_kernel,
        grid=(freqs // step,),
        in_specs=[pl.BlockSpec((step, shots, lanes), lambda g: (g, 0, 0))],
        out_specs=pl.BlockSpec((step, 2, shots, lanes // 2), lambda g: (g, 0, 0, 0)),
        out_shape=jax.ShapeDtypeStruct((freqs, 2, shots, lanes // 2), jnp.float32),
        name="output",
    )(arrived)


def local(tile_rows, tile_columns, traces, aperture_lists, aperture_counts):
    shots = traces.shape[0]
    devices = tile_rows * tile_columns
    whole = FREQS % devices == 0
    axes = ("shot", "rcv") if whole else ("shot",)
    destinations = devices if whole else tile_rows
    freqs = FREQS // destinations
    mask_rows = -(-tile_columns // 8) * 8
    sent = spectra(traces, aperture_lists, aperture_counts, destinations, mask_rows)
    held = lax.all_to_all(sent, axes, 0, 0, tiled=True)
    own = None
    if not whole:
        own = held
        held = lax.all_gather(held, "rcv", axis=0, tiled=True)
    made = products(held, own, tile_rows, tile_columns, shots, freqs)
    home = lax.all_to_all(made, axes, 0, 0, tiled=True)
    return output(home.reshape(FREQS, shots, LANES))


def solution(mesh):
    placed = (P("shot", "rcv", None), P("shot", "rcv", None), P("shot", "rcv"))
    body = functools.partial(local, mesh.shape["shot"], mesh.shape["rcv"])
    return jax.shard_map(
        body, mesh=mesh, in_specs=placed, out_specs=P(None, None, "shot", "rcv"), check_vma=False
    )
```

time: 210 us -> 56.3 us (0.27)
  waiting for transfers between devices: 71.8 us -> 0 us
  local copies, waits for them, and re-layouts: 69.7 us -> 0 us
  between operations: 14.2 us -> 0.65 us
  blocking collectives: 31 us -> 43.2 us
  Pallas kernels: 0 us -> 12 us
  other arithmetic: 8.59 us -> 0 us
  matrix products: 8.46 us -> 0 us
  starting transfers between devices: 4.85 us -> 0 us
    all_to_all x0 -> x2, blocking collectives: none -> 43.2 us  [the longest x1 24.2 us: local(): held = lax.all_to_all(sent, axes, 0, 0, tiled=True)]
    unnamed x15 -> x0, local copies, waits for them, and re-layouts: 41.3 us -> none
    all_to_all x1 -> x0, waiting for transfers between devices: 36.1 us -> none  [local(): lax.all_to_all(outgoing, 'shot', split_axis=2, concat_axis=2, tiled=True)]
    all_gather x1 -> x0, waiting for transfers between devices: 35.7 us -> none  [local(): shot_rows = lax.all_gather(trace_spectrum, 'rcv', axis=3, tiled=True)]
    all_gather x1 -> x0, blocking collectives: 17.9 us -> none  [local(): lax.all_gather(aperture_lists, 'shot', axis=0, tiled=True)]
    mul x4 -> x0, local copies, waits for them, and re-layouts: 13.7 us -> none  [the longest x3 12.2 us: local(): trace_spectrum[:, :, None, :, :] * named[None, None, :, None, None]]
    unnamed x1 -> x0, blocking collectives: 13.1 us -> none
    pallas_call x0 -> x3, Pallas kernels: none -> 12 us  [the longest x1 5.48 us: spectra(): pl.pallas_call(functools.partial(spectra_kernel, mask_rows), grid=(half /...]
  transfers between devices with their start and end apart: 2 -> 0, of which waited for: 2 -> 0; matrix products, arithmetic and copies ran while one was open for 7% -> 0% of each run, Pallas kernels for 0% -> 0%
where the time goes in v1:
time: 56.3 us; the launch traced here: 55.8 us
  blocking collectives  43.2 us (77%)
  Pallas kernels  12 us (21%)
  between operations  0.65 us (1%)
    all_to_all x1, blocking collectives, local(): held = lax.all_to_all(sent, axes, 0, 0, tiled=True)  24.2 us
    all_to_all x1, blocking collectives, local(): home = lax.all_to_all(made, axes, 0, 0, tiled=True)  18.9 us
    pallas_call x1, Pallas kernels, spectra(): pl.pallas_call(functools.partial(spectra_kernel, mask_rows), grid=(half /...  5.48 us
    pallas_call x1, Pallas kernels, output(): pl.pallas_call(output_kernel, grid=(freqs // step,), in_specs=[pl.BlockSp...  3.61 us
    pallas_call x1, Pallas kernels, products(): pl.pallas_call(functools.partial(products_kernel, tile_rows, tile_columns...  2.94 us

profile of v1, /device:TPU:0, one launch (start us, length us, event | category | flops | bytes accessed | tf_op | source)
XLA Modules:
  0.0 55.8 jit_solution(16789869958359100488)
XLA Ops:
  0.7 5.5 %spectra.1 = bf16[32,72,128]{2,1,0:T(8,128)(2,1)} custom-call(s32[1,1,8]{2,1,0:T(1,128)} %list_ref.1, s32[1,1]{1,0:T(1,128)S(6)} %copy.5.count_ref, bf16[2,16,64,1024]{3,2,1,0:T(8,128)(2,1)} %bitcast.2, bf16[128,1024]{1,0:T(8,128)(2,1)} %constant.2.clone.table_ref), custom_call_target="tpu_custom_call" | custom-call | tf_op jit(solution)/shard_map/spectra/pallas_call | solution.py:67
  6.1 24.2 %all_to_all.10.refs_0_ = bf16[32,72,128]{2,1,0:T(8,128)(2,1)} all-to-all(bf16[32,72,128]{2,1,0:T(8,128)(2,1)} %spectra.1), channel_id=1, replica_groups=mesh['shot'=8,'rcv'=4] {'shot','rcv'}, dimensions={0} | all-to-all | bytes 1179648 | tf_op jit(solution)/shard_map/all_to_all | solution.py:171
  30.4 2.9 %products.1 = bf16[32,64,128]{2,1,0:T(8,128)(2,1)} custom-call(bf16[32,72,128]{2,1,0:T(8,128)(2,1)} %all_to_all.10.refs_0_), custom_call_target="tpu_custom_call" | custom-call | tf_op jit(solution)/shard_map/products/pallas_call | solution.py:127
  33.3 18.9 %all_to_all.11 = bf16[32,64,128]{2,1,0:T(8,128)(2,1)} all-to-all(bf16[32,64,128]{2,1,0:T(8,128)(2,1)} %products.1), channel_id=1, replica_groups=mesh['shot'=8,'rcv'=4] {'shot','rcv'}, dimensions={0} | all-to-all | bytes 1048576 | tf_op jit(solution)/shard_map/all_to_all | solution.py:177
  52.2 3.6 %output.1 = f32[64,2,32,64]{3,2,1,0:T(8,128)} custom-call(bf16[64,32,128]{2,1,0:T(8,128)(2,1)} %bitcast.3), custom_call_target="tpu_custom_call" | custom-call | tf_op jit(solution)/shard_map/output/pallas_call | solution.py:152

commit v2 on v1

--- a/solution.py
+++ b/solution.py
@@ -15,6 +15,8 @@
 FREQS = 64
 APB = 8
 LANES = 128
+PITCH = 136
+GRANT = 16 << 20
 
 
 def dft_rows(samples):
@@ -24,64 +26,73 @@
     return rows.reshape(2 * FREQS, samples).astype(jnp.bfloat16)
 
 
-def spectra_kernel(mask_rows, list_ref, count_ref, traces_ref, table_ref, out_ref, held):
-    step, steps = pl.program_id(0), pl.num_programs(0)
-    group, receivers = traces_ref.shape[1], traces_ref.shape[2]
+def spectra_kernel(mask_rows, chunks, list_hbm, count_ref, traces_hbm, table_hbm, out_ref, list_ref, traces, table, held, sems):
+    half, receivers = traces.shape[1], traces.shape[2]
     destinations = out_ref.shape[0]
-    half = group * steps
-    for a in range(group):
-        pair = jnp.concatenate([traces_ref[0, a], traces_ref[1, a]], axis=0)
-        held[pl.ds((step * group + a) * LANES, LANES), :] = lax.dot_general(
-            table_ref[...], pair, (((1,), (1,)), ((), ())), preferred_element_type=jnp.float32
+    group = half // chunks
+    pitch = PITCH
+    copies = [pltpu.make_async_copy(table_hbm, table, sems.at[0])]
+    for g in range(chunks):
+        part = pl.ds(g * group, group)
+        copies.append(pltpu.make_async_copy(traces_hbm.at[:, part], traces.at[:, part], sems.at[1 + g]))
+    copies.append(pltpu.make_async_copy(list_hbm, list_ref, sems.at[1 + chunks]))
+    for copy in copies:
+        copy.start()
+    copies[0].wait()
+    for a in range(half):
+        if a % group == 0:
+            copies[1 + a // group].wait()
+        pair = jnp.concatenate([traces[0, a], traces[1, a]], axis=0)
+        held[a * pitch : a * pitch + 2 * FREQS, :] = lax.dot_general(
+            table[...], pair, (((1,), (1,)), ((), ())), preferred_element_type=jnp.float32
         )
-
-    @pl.when(step == steps - 1)
-    def _():
-        low = lax.broadcasted_iota(jnp.int32, (half, LANES), 1) < receivers
-        per = FREQS // destinations
-        for q in range(FREQS):
-            real = held[pl.ds(2 * q, half, stride=LANES), :]
-            imag = held[pl.ds(2 * q + 1, half, stride=LANES), :]
-            first = jnp.where(low, real, pltpu.roll(imag, receivers, 1))
-            second = jnp.where(low, pltpu.roll(real, receivers, 1), imag)
-            base = (q % per) * 2 * half
-            out_ref[q // per, base : base + half, :] = first.astype(jnp.bfloat16)
-            out_ref[q // per, base + half : base + 2 * half, :] = second.astype(jnp.bfloat16)
-        parts = receivers // (2 * half)
-        lane = lax.broadcasted_iota(jnp.int32, (mask_rows, LANES), 1)
-        block = lax.broadcasted_iota(jnp.int32, (mask_rows, LANES), 0) * parts + lane % receivers // (2 * half)
-        member = jnp.zeros((mask_rows, LANES), jnp.float32)
-        for slot in range(APB):
-            live = jnp.logical_and(block == list_ref[0, 0, slot], slot < count_ref[0, 0])
-            member = jnp.where(live, 1.0, member)
-        member = member.astype(jnp.bfloat16)
-        for d in range(destinations):
-            out_ref[d, per * 2 * half :, :] = member
+    copies[-1].wait()
+    low = lax.broadcasted_iota(jnp.int32, (half, LANES), 1) < receivers
+    per = FREQS // destinations
+    for q in range(FREQS):
+        real = held[pl.ds(2 * q, half, stride=pitch), :]
+        imag = held[pl.ds(2 * q + 1, half, stride=pitch), :]
+        first = jnp.where(low, real, pltpu.roll(imag, receivers, 1))
+        second = jnp.where(low, pltpu.roll(real, receivers, 1), imag)
+        base = (q % per) * 2 * half
+        out_ref[q // per, base : base + half, :] = first.astype(jnp.bfloat16)
+        out_ref[q // per, base + half : base + 2 * half, :] = second.astype(jnp.bfloat16)
+    parts = receivers // (2 * half)
+    lane = lax.broadcasted_iota(jnp.int32, (mask_rows, LANES), 1)
+    block = lax.broadcasted_iota(jnp.int32, (mask_rows, LANES), 0) * parts + lane % receivers // (2 * half)
+    member = jnp.zeros((mask_rows, LANES), jnp.float32)
+    for slot in range(APB):
+        live = jnp.logical_and(block == list_ref[0, 0, slot], slot < count_ref[0, 0])
+        member = jnp.where(live, 1.0, member)
+    member = member.astype(jnp.bfloat16)
+    for d in range(destinations):
+        out_ref[d, per * 2 * half :, :] = member
 
 
 def spectra(traces, aperture_lists, aperture_counts, destinations, mask_rows):
     shots, receivers, samples = traces.shape
     half = shots // 2
-    group = 4
+    chunks = 4
     rows = FREQS // destinations * shots + mask_rows
     return pl.pallas_call(
-        functools.partial(spectra_kernel, mask_rows),
-        grid=(half // group,),
-        in_specs=[
-            pl.BlockSpec(memory_space=pltpu.SMEM),
-            pl.BlockSpec(memory_space=pltpu.SMEM),
-            pl.BlockSpec((2, group, receivers, samples), lambda g: (0, g, 0, 0)),
-            pl.BlockSpec((2 * FREQS, samples), lambda g: (0, 0)),
+        functools.partial(spectra_kernel, mask_rows, chunks),
+        in_specs=[pl.BlockSpec(memory_space=pltpu.SMEM if k == 1 else pltpu.HBM) for k in range(4)],
+        out_specs=pl.BlockSpec(memory_space=pltpu.VMEM),
+        out_shape=jax.ShapeDtypeStruct((destinations, rows, LANES), jnp.bfloat16),
+        scratch_shapes=[
+            pltpu.SMEM(aperture_lists.shape, jnp.int32),
+            pltpu.VMEM((2, half, receivers, samples), jnp.bfloat16),
+            pltpu.VMEM((2 * FREQS, samples), jnp.bfloat16),
+            pltpu.VMEM((half * PITCH, LANES), jnp.float32),
+            pltpu.SemaphoreType.DMA((chunks + 2,)),
         ],
-        out_specs=pl.BlockSpec((destinations, rows, LANES), lambda g: (0, 0, 0)),
-        out_shape=jax.ShapeDtypeStruct((destinations, rows, LANES), jnp.bfloat16),
-        scratch_shapes=[pltpu.VMEM((half * LANES, LANES), jnp.float32)],
+        compiler_params=pltpu.CompilerParams(vmem_limit_bytes=GRANT),
         name="spectra",
     )(
-        aperture_lists,
+        pltpu.with_memory_space_constraint(aperture_lists, pltpu.HBM),
         aperture_counts,
-        traces.reshape(2, half, receivers, samples),
-        jnp.asarray(dft_rows(samples)),
+        pltpu.with_memory_space_constraint(traces.reshape(2, half, receivers, samples), pltpu.HBM),
+        pltpu.with_memory_space_constraint(jnp.asarray(dft_rows(samples)), pltpu.HBM),
     )
 
 
@@ -135,6 +146,7 @@
             pltpu.VMEM((columns, tile_rows * shots, tile_columns * LANES), jnp.bfloat16),
             pltpu.VMEM((columns, tile_columns * LANES, LANES), jnp.bfloat16),
         ],
+        compiler_params=pltpu.CompilerParams(vmem_limit_bytes=GRANT),
         name="products",
     )(*operands)
 
@@ -155,6 +167,7 @@
         in_specs=[pl.BlockSpec((step, shots, lanes), lambda g: (g, 0, 0))],
         out_specs=pl.BlockSpec((step, 2, shots, lanes // 2), lambda g: (g, 0, 0, 0)),
         out_shape=jax.ShapeDtypeStruct((freqs, 2, shots, lanes // 2), jnp.float32),
+        compiler_params=pltpu.CompilerParams(vmem_limit_bytes=GRANT),
         name="output",
     )(arrived)
 

time: 56.3 us -> 49.9 us (0.89)
  Pallas kernels: 12 us -> 6.47 us
  blocking collectives: 43.2 us -> 42.5 us
    pallas_call x1, Pallas kernels: 5.48 us -> 3.4 us  [spectra(): pl.pallas_call(functools.partial(spectra_kernel, mask_rows, chunks), in_s...]
    pallas_call x1, Pallas kernels: 2.94 us -> 1.1 us  [products(): pl.pallas_call(functools.partial(products_kernel, tile_rows, tile_columns...]
    pallas_call x1, Pallas kernels: 3.61 us -> 1.97 us  [output(): pl.pallas_call(output_kernel, grid=(freqs // step,), in_specs=[pl.BlockSp...]
where the time goes in v2:
time: 49.9 us; the launch traced here: 49.7 us
  blocking collectives  42.5 us (85%)
  Pallas kernels  6.47 us (13%)
  between operations  0.67 us (1%)
    all_to_all x1, blocking collectives, local(): held = lax.all_to_all(sent, axes, 0, 0, tiled=True)  23.9 us
    all_to_all x1, blocking collectives, local(): home = lax.all_to_all(made, axes, 0, 0, tiled=True)  18.6 us
    pallas_call x1, Pallas kernels, spectra(): pl.pallas_call(functools.partial(spectra_kernel, mask_rows, chunks), in_s...  3.4 us
    pallas_call x1, Pallas kernels, output(): pl.pallas_call(output_kernel, grid=(freqs // step,), in_specs=[pl.BlockSp...  1.97 us
    pallas_call x1, Pallas kernels, products(): pl.pallas_call(functools.partial(products_kernel, tile_rows, tile_columns...  1.1 us

profile of v2, /device:TPU:0, one launch (start us, length us, event | category | flops | bytes accessed | tf_op | source)
XLA Modules:
  0.0 49.7 jit_solution(6171407989067715053)
XLA Ops:
  0.7 3.4 %spectra.1 = bf16[32,72,128]{2,1,0:T(8,128)(2,1)S(1)} custom-call(s32[1,1,8]{2,1,0:T(1,128)} %list_hbm.1, s32[1,1]{1,0:T(1,128)S(6)} %copy.5.count_ref, bf16[2,16,64,1024]{3,2,1,0:T(8,128)(2,1)} %bitcast.3, bf16[128,1024]{1,0:T(8,128)(2,1)} %constant.2.clone.table_hbm), custom_call_target="tpu_custom_call" | custom-call | tf_op jit(solution)/shard_map/spectra/pallas_call | solution.py:77
  4.1 23.9 %all_to_all.10.refs_0_ = bf16[32,72,128]{2,1,0:T(8,128)(2,1)S(1)} all-to-all(bf16[32,72,128]{2,1,0:T(8,128)(2,1)S(1)} %spectra.1), channel_id=1, replica_groups=mesh['shot'=8,'rcv'=4] {'shot','rcv'}, dimensions={0} | all-to-all | bytes 1179648 | tf_op jit(solution)/shard_map/all_to_all | solution.py:184
  28.0 1.1 %products.1 = bf16[32,64,128]{2,1,0:T(8,128)(2,1)S(1)} custom-call(bf16[32,72,128]{2,1,0:T(8,128)(2,1)S(1)} %all_to_all.10.refs_0_), custom_call_target="tpu_custom_call" | custom-call | tf_op jit(solution)/shard_map/products/pallas_call | solution.py:138
  29.1 18.6 %all_to_all.11 = bf16[32,64,128]{2,1,0:T(8,128)(2,1)S(1)} all-to-all(bf16[32,64,128]{2,1,0:T(8,128)(2,1)S(1)} %products.1), channel_id=1, replica_groups=mesh['shot'=8,'rcv'=4] {'shot','rcv'}, dimensions={0} | all-to-all | bytes 1048576 | tf_op jit(solution)/shard_map/all_to_all | solution.py:190
  47.7 2.0 %output.1 = f32[64,2,32,64]{3,2,1,0:T(8,128)} custom-call(bf16[64,32,128]{2,1,0:T(8,128)(2,1)S(1)} %bitcast.2), custom_call_target="tpu_custom_call" | custom-call | tf_op jit(solution)/shard_map/output/pallas_call | solution.py:164

commit v3 on v2

--- a/solution.py
+++ b/solution.py
@@ -151,22 +151,32 @@
     )(*operands)
 
 
-def output_kernel(in_ref, out_ref):
-    receivers = out_ref.shape[3]
-    block = in_ref[...].astype(jnp.float32)
-    out_ref[:, 0] = block[:, :, :receivers]
-    out_ref[:, 1] = block[:, :, receivers:]
+def output_kernel(chunks, in_ref, out_ref, held, sems):
+    freqs, receivers = in_ref.shape[0], out_ref.shape[3]
+    step = freqs // chunks
+    copies = []
+    for g in range(chunks):
+        part = slice(g * step, (g + 1) * step)
+        block = in_ref[part].astype(jnp.float32)
+        held[part, 0] = block[:, :, :receivers]
+        held[part, 1] = block[:, :, receivers:]
+        copy = pltpu.make_async_copy(held.at[part], out_ref.at[part], sems.at[g])
+        copy.start()
+        copies.append(copy)
+    for copy in copies:
+        copy.wait()
 
 
 def output(arrived):
     freqs, shots, lanes = arrived.shape
-    step = 16
+    chunks = 4
+    shape = (freqs, 2, shots, lanes // 2)
     return pl.pallas_call(
-        output_kernel,
-        grid=(freqs // step,),
-        in_specs=[pl.BlockSpec((step, shots, lanes), lambda g: (g, 0, 0))],
-        out_specs=pl.BlockSpec((step, 2, shots, lanes // 2), lambda g: (g, 0, 0, 0)),
-        out_shape=jax.ShapeDtypeStruct((freqs, 2, shots, lanes // 2), jnp.float32),
+        functools.partial(output_kernel, chunks),
+        in_specs=[pl.BlockSpec(memory_space=pltpu.VMEM)],
+        out_specs=pl.BlockSpec(memory_space=pltpu.HBM),
+        out_shape=jax.ShapeDtypeStruct(shape, jnp.float32),
+        scratch_shapes=[pltpu.VMEM(shape, jnp.float32), pltpu.SemaphoreType.DMA((chunks,))],
         compiler_params=pltpu.CompilerParams(vmem_limit_bytes=GRANT),
         name="output",
     )(arrived)

time: 49.9 us -> 49.4 us (0.990)
  Pallas kernels: 6.47 us -> 5.95 us
    pallas_call x1, Pallas kernels: 1.97 us -> 1.45 us  [output(): pl.pallas_call(functools.partial(output_kernel, chunks), in_specs=[pl.Blo...]
where the time goes in v3:
time: 49.4 us; the launch traced here: 49.2 us
  blocking collectives  42.5 us (86%)
  Pallas kernels  5.95 us (12%)
  between operations  0.67 us (1%)
    all_to_all x1, blocking collectives, local(): held = lax.all_to_all(sent, axes, 0, 0, tiled=True)  23.9 us
    all_to_all x1, blocking collectives, local(): home = lax.all_to_all(made, axes, 0, 0, tiled=True)  18.6 us
    pallas_call x1, Pallas kernels, spectra(): pl.pallas_call(functools.partial(spectra_kernel, mask_rows, chunks), in_s...  3.4 us
    pallas_call x1, Pallas kernels, output(): pl.pallas_call(functools.partial(output_kernel, chunks), in_specs=[pl.Blo...  1.45 us
    pallas_call x1, Pallas kernels, products(): pl.pallas_call(functools.partial(products_kernel, tile_rows, tile_columns...  1.1 us

profile of v3, /device:TPU:0, one launch (start us, length us, event | category | flops | bytes accessed | tf_op | source)
XLA Modules:
  0.0 49.2 jit_solution(17461632978176812340)
XLA Ops:
  0.7 3.4 %spectra.1 = bf16[32,72,128]{2,1,0:T(8,128)(2,1)S(1)} custom-call(s32[1,1,8]{2,1,0:T(1,128)} %list_hbm.1, s32[1,1]{1,0:T(1,128)S(6)} %copy.5.count_ref, bf16[2,16,64,1024]{3,2,1,0:T(8,128)(2,1)} %bitcast.3, bf16[128,1024]{1,0:T(8,128)(2,1)} %constant.2.clone.table_hbm), custom_call_target="tpu_custom_call" | custom-call | tf_op jit(solution)/shard_map/spectra/pallas_call | solution.py:77
  4.1 23.9 %all_to_all.10.refs_0_ = bf16[32,72,128]{2,1,0:T(8,128)(2,1)S(1)} all-to-all(bf16[32,72,128]{2,1,0:T(8,128)(2,1)S(1)} %spectra.1), channel_id=1, replica_groups=mesh['shot'=8,'rcv'=4] {'shot','rcv'}, dimensions={0} | all-to-all | bytes 1179648 | tf_op jit(solution)/shard_map/all_to_all | solution.py:194
  28.0 1.1 %products.1 = bf16[32,64,128]{2,1,0:T(8,128)(2,1)S(1)} custom-call(bf16[32,72,128]{2,1,0:T(8,128)(2,1)S(1)} %all_to_all.10.refs_0_), custom_call_target="tpu_custom_call" | custom-call | tf_op jit(solution)/shard_map/products/pallas_call | solution.py:138
  29.1 18.6 %all_to_all.11 = bf16[32,64,128]{2,1,0:T(8,128)(2,1)S(1)} all-to-all(bf16[32,64,128]{2,1,0:T(8,128)(2,1)S(1)} %products.1), channel_id=1, replica_groups=mesh['shot'=8,'rcv'=4] {'shot','rcv'}, dimensions={0} | all-to-all | bytes 1048576 | tf_op jit(solution)/shard_map/all_to_all | solution.py:200
  47.7 1.4 %output.1 = f32[64,2,32,64]{3,2,1,0:T(8,128)} custom-call(bf16[64,32,128]{2,1,0:T(8,128)(2,1)S(1)} %bitcast.2), custom_call_target="tpu_custom_call" | custom-call | tf_op jit(solution)/shard_map/output/pallas_call | solution.py:174

commit v4 on v3

--- a/solution.py
+++ b/solution.py
@@ -98,12 +98,12 @@
 
 def products_kernel(tile_rows, tile_columns, own, shots, scale, *refs):
     if own:
-        left_ref, right_ref, out_ref, left, right = refs
+        left_ref, right_ref, out_ref, right = refs
         columns, right_of = (0,), lambda i, j: i
         left_of = lambda i, j: j * tile_rows + i
         out_of = lambda i, j: i
     else:
-        left_ref, out_ref, left, right = refs
+        left_ref, out_ref, right = refs
         right_ref = left_ref
         columns = range(tile_columns)
         left_of = right_of = out_of = lambda i, j: i * tile_columns + j
@@ -111,21 +111,31 @@
     parts = receivers // shots
     freqs = out_ref.shape[1] // shots
     sign = jnp.where(lax.broadcasted_iota(jnp.int32, (shots, LANES), 1) < receivers, -1.0, 1.0)
+    sign = sign.astype(jnp.bfloat16)
     for q in range(freqs):
         rows = slice(q * shots, (q + 1) * shots)
         for j in columns:
+            at = q * len(columns) + j
             for b in range(tile_rows):
                 block = right_ref[right_of(b, j), rows, :]
-                turned = pltpu.roll(block.astype(jnp.float32), receivers, 1) * sign
+                turned = pltpu.roll(block, receivers, 1) * sign
                 base = b // parts * LANES + b % parts * shots
-                right[j, base : base + shots, :] = block
-                right[j, base + receivers : base + receivers + shots, :] = turned.astype(jnp.bfloat16)
-            for i in range(tile_rows):
-                for k in range(tile_columns):
-                    m = freqs * shots + k
-                    member = right_ref[right_of(i, j), m : m + 1, :]
-                    left[j, i * shots : (i + 1) * shots, k * LANES : (k + 1) * LANES] = left_ref[left_of(i, k), rows, :] * member
-            total = jnp.dot(left[j], right[j], preferred_element_type=jnp.float32) * scale
+                right[at, base : base + shots, :] = block
+                right[at, base + receivers : base + receivers + shots, :] = turned
+    for q in range(freqs):
+        rows = slice(q * shots, (q + 1) * shots)
+        for j in columns:
+            at = q * len(columns) + j
+            masked = []
+            for k in range(tile_columns):
+                m = freqs * shots + k
+                tiles = [
+                    left_ref[left_of(i, k), rows, :] * right_ref[right_of(i, j), m : m + 1, :]
+                    for i in range(tile_rows)
+                ]
+                masked.append(jnp.concatenate(tiles, axis=0))
+            masked = jnp.concatenate(masked, axis=1)
+            total = jnp.dot(masked, right[at], preferred_element_type=jnp.float32) * scale
             total = total.astype(jnp.bfloat16)
             for i in range(tile_rows):
                 out_ref[out_of(i, j), rows, :] = total[i * shots : (i + 1) * shots, :]
@@ -143,8 +153,7 @@
         in_specs=[pl.BlockSpec(memory_space=pltpu.VMEM)] * len(operands),
         out_specs=pl.BlockSpec(memory_space=pltpu.VMEM),
         scratch_shapes=[
-            pltpu.VMEM((columns, tile_rows * shots, tile_columns * LANES), jnp.bfloat16),
-            pltpu.VMEM((columns, tile_columns * LANES, LANES), jnp.bfloat16),
+            pltpu.VMEM((freqs * columns, tile_columns * LANES, LANES), jnp.bfloat16),
         ],
         compiler_params=pltpu.CompilerParams(vmem_limit_bytes=GRANT),
         name="products",

time: 49.4 us -> 49 us (level)
  no operation moved by 1% of the time
where the time goes in v4:
time: 49 us; the launch traced here: 48.9 us
  blocking collectives  42.5 us (87%)
  Pallas kernels  5.65 us (12%)
  between operations  0.67 us (1%)
    all_to_all x1, blocking collectives, local(): held = lax.all_to_all(sent, axes, 0, 0, tiled=True)  23.9 us
    all_to_all x1, blocking collectives, local(): home = lax.all_to_all(made, axes, 0, 0, tiled=True)  18.6 us
    pallas_call x1, Pallas kernels, spectra(): pl.pallas_call(functools.partial(spectra_kernel, mask_rows, chunks), in_s...  3.4 us
    pallas_call x1, Pallas kernels, output(): pl.pallas_call(functools.partial(output_kernel, chunks), in_specs=[pl.Blo...  1.45 us

profile of v4, /device:TPU:0, one launch (start us, length us, event | category | flops | bytes accessed | tf_op | source)
XLA Modules:
  0.0 48.9 jit_solution(17075404264729148968)
XLA Ops:
  0.7 3.4 %spectra.1 = bf16[32,72,128]{2,1,0:T(8,128)(2,1)S(1)} custom-call(s32[1,1,8]{2,1,0:T(1,128)} %list_hbm.1, s32[1,1]{1,0:T(1,128)S(6)} %copy.5.count_ref, bf16[2,16,64,1024]{3,2,1,0:T(8,128)(2,1)} %bitcast.3, bf16[128,1024]{1,0:T(8,128)(2,1)} %constant.2.clone.table_hbm), custom_call_target="tpu_custom_call" | custom-call | tf_op jit(solution)/shard_map/spectra/pallas_call | solution.py:77
  4.1 23.9 %all_to_all.10.refs_0_ = bf16[32,72,128]{2,1,0:T(8,128)(2,1)S(1)} all-to-all(bf16[32,72,128]{2,1,0:T(8,128)(2,1)S(1)} %spectra.1), channel_id=1, replica_groups=mesh['shot'=8,'rcv'=4] {'shot','rcv'}, dimensions={0} | all-to-all | bytes 1179648 | tf_op jit(solution)/shard_map/all_to_all | solution.py:203
  28.0 0.8 %products.1 = bf16[32,64,128]{2,1,0:T(8,128)(2,1)S(1)} custom-call(bf16[32,72,128]{2,1,0:T(8,128)(2,1)S(1)} %all_to_all.10.refs_0_), custom_call_target="tpu_custom_call" | custom-call | tf_op jit(solution)/shard_map/products/pallas_call | solution.py:148
  28.8 18.6 %all_to_all.11 = bf16[32,64,128]{2,1,0:T(8,128)(2,1)S(1)} all-to-all(bf16[32,64,128]{2,1,0:T(8,128)(2,1)S(1)} %products.1), channel_id=1, replica_groups=mesh['shot'=8,'rcv'=4] {'shot','rcv'}, dimensions={0} | all-to-all | bytes 1048576 | tf_op jit(solution)/shard_map/all_to_all | solution.py:209
  47.4 1.4 %output.1 = f32[64,2,32,64]{3,2,1,0:T(8,128)} custom-call(bf16[64,32,128]{2,1,0:T(8,128)(2,1)S(1)} %bitcast.2), custom_call_target="tpu_custom_call" | custom-call | tf_op jit(solution)/shard_map/output/pallas_call | solution.py:183

commit v5 on v4

--- a/solution.py
+++ b/solution.py
@@ -26,9 +26,9 @@
     return rows.reshape(2 * FREQS, samples).astype(jnp.bfloat16)
 
 
-def spectra_kernel(mask_rows, chunks, list_hbm, count_ref, traces_hbm, table_hbm, out_ref, list_ref, traces, table, held, sems):
+def spectra_kernel(destinations, mask_rows, chunks, list_hbm, count_ref, traces_hbm, table_hbm, out_ref, list_ref, traces, table, held, sems):
     half, receivers = traces.shape[1], traces.shape[2]
-    destinations = out_ref.shape[0]
+    rows = out_ref.shape[0] // destinations
     group = half // chunks
     pitch = PITCH
     copies = [pltpu.make_async_copy(table_hbm, table, sems.at[0])]
@@ -54,9 +54,9 @@
         imag = held[pl.ds(2 * q + 1, half, stride=pitch), :]
         first = jnp.where(low, real, pltpu.roll(imag, receivers, 1))
         second = jnp.where(low, pltpu.roll(real, receivers, 1), imag)
-        base = (q % per) * 2 * half
-        out_ref[q // per, base : base + half, :] = first.astype(jnp.bfloat16)
-        out_ref[q // per, base + half : base + 2 * half, :] = second.astype(jnp.bfloat16)
+        base = q // per * rows + q % per * 2 * half
+        out_ref[base : base + half, :] = first.astype(jnp.bfloat16)
+        out_ref[base + half : base + 2 * half, :] = second.astype(jnp.bfloat16)
     parts = receivers // (2 * half)
     lane = lax.broadcasted_iota(jnp.int32, (mask_rows, LANES), 1)
     block = lax.broadcasted_iota(jnp.int32, (mask_rows, LANES), 0) * parts + lane % receivers // (2 * half)
@@ -66,7 +66,7 @@
         member = jnp.where(live, 1.0, member)
     member = member.astype(jnp.bfloat16)
     for d in range(destinations):
-        out_ref[d, per * 2 * half :, :] = member
+        out_ref[(d + 1) * rows - mask_rows : (d + 1) * rows, :] = member
 
 
 def spectra(traces, aperture_lists, aperture_counts, destinations, mask_rows):
@@ -75,10 +75,10 @@
     chunks = 4
     rows = FREQS // destinations * shots + mask_rows
     return pl.pallas_call(
-        functools.partial(spectra_kernel, mask_rows, chunks),
+        functools.partial(spectra_kernel, destinations, mask_rows, chunks),
         in_specs=[pl.BlockSpec(memory_space=pltpu.SMEM if k == 1 else pltpu.HBM) for k in range(4)],
         out_specs=pl.BlockSpec(memory_space=pltpu.VMEM),
-        out_shape=jax.ShapeDtypeStruct((destinations, rows, LANES), jnp.bfloat16),
+        out_shape=jax.ShapeDtypeStruct((destinations * rows, LANES), jnp.bfloat16),
         scratch_shapes=[
             pltpu.SMEM(aperture_lists.shape, jnp.int32),
             pltpu.VMEM((2, half, receivers, samples), jnp.bfloat16),
@@ -96,65 +96,71 @@
     )
 
 
-def products_kernel(tile_rows, tile_columns, own, shots, scale, *refs):
+def products_kernel(tile_rows, tile_columns, own, shots, mask_rows, scale, *refs):
     if own:
         left_ref, right_ref, out_ref, right = refs
         columns, right_of = (0,), lambda i, j: i
-        left_of = lambda i, j: j * tile_rows + i
-        out_of = lambda i, j: i
     else:
-        left_ref, out_ref, right = refs
-        right_ref = left_ref
-        columns = range(tile_columns)
-        left_of = right_of = out_of = lambda i, j: i * tile_columns + j
+        right_ref, out_ref, right = refs
+        columns, right_of = range(tile_columns), lambda i, j: i * tile_columns + j
     receivers = LANES // 2
     parts = receivers // shots
     freqs = out_ref.shape[1] // shots
+    rows = freqs * shots + mask_rows
     sign = jnp.where(lax.broadcasted_iota(jnp.int32, (shots, LANES), 1) < receivers, -1.0, 1.0)
     sign = sign.astype(jnp.bfloat16)
+    places = [b // parts * LANES + b % parts * shots for b in range(tile_rows)]
+
+    def left_block(q, i, k):
+        if own:
+            base = (k * tile_rows + i) * rows + q * shots
+            return left_ref[base : base + shots, :]
+        return right[q * tile_columns + k, places[i] : places[i] + shots, :]
+
     for q in range(freqs):
-        rows = slice(q * shots, (q + 1) * shots)
         for j in columns:
             at = q * len(columns) + j
             for b in range(tile_rows):
-                block = right_ref[right_of(b, j), rows, :]
+                base = right_of(b, j) * rows + q * shots
+                block = right_ref[base : base + shots, :]
                 turned = pltpu.roll(block, receivers, 1) * sign
-                base = b // parts * LANES + b % parts * shots
-                right[at, base : base + shots, :] = block
-                right[at, base + receivers : base + receivers + shots, :] = turned
+                right[at, places[b] : places[b] + shots, :] = block
+                right[at, places[b] + receivers : places[b] + receivers + shots, :] = turned
     for q in range(freqs):
-        rows = slice(q * shots, (q + 1) * shots)
         for j in columns:
-            at = q * len(columns) + j
             masked = []
             for k in range(tile_columns):
-                m = freqs * shots + k
-                tiles = [
-                    left_ref[left_of(i, k), rows, :] * right_ref[right_of(i, j), m : m + 1, :]
-                    for i in range(tile_rows)
-                ]
+                tiles = []
+                for i in range(tile_rows):
+                    m = right_of(i, j) * rows + freqs * shots + k
+                    tiles.append(left_block(q, i, k) * right_ref[m : m + 1, :])
                 masked.append(jnp.concatenate(tiles, axis=0))
             masked = jnp.concatenate(masked, axis=1)
-            total = jnp.dot(masked, right[at], preferred_element_type=jnp.float32) * scale
+            total = jnp.dot(
+                masked, right[q * len(columns) + j], preferred_element_type=jnp.float32
+            ) * scale
             total = total.astype(jnp.bfloat16)
             for i in range(tile_rows):
-                out_ref[out_of(i, j), rows, :] = total[i * shots : (i + 1) * shots, :]
-
-
-def products(left, right, tile_rows, tile_columns, shots, freqs):
-    own = right is not None
-    operands = (left, right) if own else (left,)
-    columns = 1 if own else tile_columns
+                out_ref[right_of(i, j), q * shots : (q + 1) * shots, :] = total[i * shots : (i + 1) * shots, :]
+
+
+def products(held, own, tile_rows, tile_columns, shots, freqs, mask_rows):
+    operands = (held,) if own is None else (held, own)
+    columns = tile_columns if own is None else 1
     return pl.pallas_call(
         functools.partial(
-            products_kernel, tile_rows, tile_columns, own, shots, 1.0 / math.sqrt(APB * shots)
+            products_kernel,
+            tile_rows,
+            tile_columns,
+            own is not None,
+            shots,
+            mask_rows,
+            1.0 / math.sqrt(APB * shots),
         ),
         out_shape=jax.ShapeDtypeStruct((tile_rows * columns, freqs * shots, LANES), jnp.bfloat16),
         in_specs=[pl.BlockSpec(memory_space=pltpu.VMEM)] * len(operands),
         out_specs=pl.BlockSpec(memory_space=pltpu.VMEM),
-        scratch_shapes=[
-            pltpu.VMEM((freqs * columns, tile_columns * LANES, LANES), jnp.bfloat16),
-        ],
+        scratch_shapes=[pltpu.VMEM((freqs * columns, tile_columns * LANES, LANES), jnp.bfloat16)],
         compiler_params=pltpu.CompilerParams(vmem_limit_bytes=GRANT),
         name="products",
     )(*operands)
@@ -198,14 +204,15 @@
     axes = ("shot", "rcv") if whole else ("shot",)
     destinations = devices if whole else tile_rows
     freqs = FREQS // destinations
-    mask_rows = -(-tile_columns // 8) * 8
+    mask_rows = tile_columns + tile_columns % 2
+    unit = math.gcd(freqs * shots + mask_rows, 8)
     sent = spectra(traces, aperture_lists, aperture_counts, destinations, mask_rows)
-    held = lax.all_to_all(sent, axes, 0, 0, tiled=True)
+    held = lax.all_to_all(sent.reshape(-1, unit, LANES), axes, 0, 0, tiled=True).reshape(-1, LANES)
     own = None
     if not whole:
         own = held
         held = lax.all_gather(held, "rcv", axis=0, tiled=True)
-    made = products(held, own, tile_rows, tile_columns, shots, freqs)
+    made = products(held, own, tile_rows, tile_columns, shots, freqs, mask_rows)
     home = lax.all_to_all(made, axes, 0, 0, tiled=True)
     return output(home.reshape(FREQS, shots, LANES))
 

time: 49 us -> 48.5 us (0.990)
  blocking collectives: 42.5 us -> 41.8 us
    all_to_all x1, blocking collectives: 23.9 us -> 23.3 us  [local(): lax.all_to_all(sent.reshape(-1, unit, LANES), axes, 0, 0, tiled=True)]
where the time goes in v5:
time: 48.5 us; the launch traced here: 48.3 us
  blocking collectives  41.8 us (86%)
  Pallas kernels  5.83 us (12%)
  between operations  0.67 us (1%)
    all_to_all x1, blocking collectives, local(): lax.all_to_all(sent.reshape(-1, unit, LANES), axes, 0, 0, tiled=True)  23.3 us
    all_to_all x1, blocking collectives, local(): home = lax.all_to_all(made, axes, 0, 0, tiled=True)  18.5 us
    pallas_call x1, Pallas kernels, spectra(): pl.pallas_call(functools.partial(spectra_kernel, destinations, mask_rows,...  3.44 us
    pallas_call x1, Pallas kernels, output(): pl.pallas_call(functools.partial(output_kernel, chunks), in_specs=[pl.Blo...  1.45 us

profile of v5, /device:TPU:0, one launch (start us, length us, event | category | flops | bytes accessed | tf_op | source)
XLA Modules:
  0.0 48.3 jit_solution(16480666746686728488)
XLA Ops:
  0.7 3.4 %spectra.1 = bf16[2176,128]{1,0:T(8,128)(2,1)S(1)} custom-call(s32[1,1,8]{2,1,0:T(1,128)} %list_hbm.1, s32[1,1]{1,0:T(1,128)S(6)} %copy.5.count_ref, bf16[2,16,64,1024]{3,2,1,0:T(8,128)(2,1)} %bitcast.7, bf16[128,1024]{1,0:T(8,128)(2,1)} %constant.2.clone.table_hbm), custom_call_target="tpu_custom_call" | custom-call | tf_op jit(solution)/shard_map/spectra/pallas_call | solution.py:77
  4.1 23.3 %all_to_all.10 = bf16[544,4,128]{2,1,0:T(4,128)(2,1)S(1)} all-to-all(bf16[544,4,128]{2,1,0:T(4,128)(2,1)S(1)} %bitcast.5), channel_id=1, replica_groups=mesh['shot'=8,'rcv'=4] {'shot','rcv'}, dimensions={0} | all-to-all | bytes 1114112 | tf_op jit(solution)/shard_map/all_to_all | solution.py:210
  27.4 0.9 %products.1 = bf16[32,64,128]{2,1,0:T(8,128)(2,1)S(1)} custom-call(bf16[2176,128]{1,0:T(8,128)(2,1)S(1)} %bitcast.4), custom_call_target="tpu_custom_call" | custom-call | tf_op jit(solution)/shard_map/products/pallas_call | solution.py:150
  28.4 18.5 %all_to_all.11 = bf16[32,64,128]{2,1,0:T(8,128)(2,1)S(1)} all-to-all(bf16[32,64,128]{2,1,0:T(8,128)(2,1)S(1)} %products.1), channel_id=1, replica_groups=mesh['shot'=8,'rcv'=4] {'shot','rcv'}, dimensions={0} | all-to-all | bytes 1048576 | tf_op jit(solution)/shard_map/all_to_all | solution.py:216
  46.9 1.4 %output.1 = f32[64,2,32,64]{3,2,1,0:T(8,128)} custom-call(bf16[64,32,128]{2,1,0:T(8,128)(2,1)S(1)} %bitcast.6), custom_call_target="tpu_custom_call" | custom-call | tf_op jit(solution)/shard_map/output/pallas_call | solution.py:189

commit v6 on v5

--- a/solution.py
+++ b/solution.py
@@ -57,9 +57,7 @@
         base = q // per * rows + q % per * 2 * half
         out_ref[base : base + half, :] = first.astype(jnp.bfloat16)
         out_ref[base + half : base + 2 * half, :] = second.astype(jnp.bfloat16)
-    parts = receivers // (2 * half)
-    lane = lax.broadcasted_iota(jnp.int32, (mask_rows, LANES), 1)
-    block = lax.broadcasted_iota(jnp.int32, (mask_rows, LANES), 0) * parts + lane % receivers // (2 * half)
+    block = lax.broadcasted_iota(jnp.int32, (mask_rows, LANES), 1)
     member = jnp.zeros((mask_rows, LANES), jnp.float32)
     for slot in range(APB):
         live = jnp.logical_and(block == list_ref[0, 0, slot], slot < count_ref[0, 0])
@@ -117,6 +115,16 @@
             return left_ref[base : base + shots, :]
         return right[q * tile_columns + k, places[i] : places[i] + shots, :]
 
+    sources = tile_rows * len(columns)
+    packed = [right_ref[t * rows + freqs * shots : t * rows + freqs * shots + 1, :] for t in range(sources)]
+    lane = lax.broadcasted_iota(jnp.int32, (LANES, tile_columns * LANES), 1)
+    block = lane // LANES * parts + lane % receivers // shots
+    chosen = lax.broadcasted_iota(jnp.int32, block.shape, 0) == block
+    spread = jnp.dot(
+        jnp.concatenate(packed, axis=0),
+        jnp.where(chosen, 1.0, 0.0).astype(jnp.bfloat16),
+        preferred_element_type=jnp.float32,
+    ).astype(jnp.bfloat16)
     for q in range(freqs):
         for j in columns:
             at = q * len(columns) + j
@@ -132,8 +140,9 @@
             for k in range(tile_columns):
                 tiles = []
                 for i in range(tile_rows):
-                    m = right_of(i, j) * rows + freqs * shots + k
-                    tiles.append(left_block(q, i, k) * right_ref[m : m + 1, :])
+                    t = right_of(i, j)
+                    member = spread[t : t + 1, k * LANES : (k + 1) * LANES]
+                    tiles.append(left_block(q, i, k) * member)
                 masked.append(jnp.concatenate(tiles, axis=0))
             masked = jnp.concatenate(masked, axis=1)
             total = jnp.dot(
@@ -204,7 +213,7 @@
     axes = ("shot", "rcv") if whole else ("shot",)
     destinations = devices if whole else tile_rows
     freqs = FREQS // destinations
-    mask_rows = tile_columns + tile_columns % 2
+    mask_rows = 2
     unit = math.gcd(freqs * shots + mask_rows, 8)
     sent = spectra(traces, aperture_lists, aperture_counts, destinations, mask_rows)
     held = lax.all_to_all(sent.reshape(-1, unit, LANES), axes, 0, 0, tiled=True).reshape(-1, LANES)

time: 48.5 us -> 48.3 us (level)
  no operation moved by 1% of the time
where the time goes in v6:
time: 48.3 us; the launch traced here: 48.1 us
  blocking collectives  41.5 us (86%)
  Pallas kernels  5.92 us (12%)
  between operations  0.67 us (1%)
    all_to_all x1, blocking collectives, local(): lax.all_to_all(sent.reshape(-1, unit, LANES), axes, 0, 0, tiled=True)  23 us
    all_to_all x1, blocking collectives, local(): home = lax.all_to_all(made, axes, 0, 0, tiled=True)  18.5 us
    pallas_call x1, Pallas kernels, spectra(): pl.pallas_call(functools.partial(spectra_kernel, destinations, mask_rows,...  3.46 us
    pallas_call x1, Pallas kernels, output(): pl.pallas_call(functools.partial(output_kernel, chunks), in_specs=[pl.Blo...  1.45 us
    pallas_call x1, Pallas kernels, products(): pl.pallas_call(functools.partial(products_kernel, tile_rows, tile_columns...  1.01 us

profile of v6, /device:TPU:0, one launch (start us, length us, event | category | flops | bytes accessed | tf_op | source)
XLA Modules:
  0.0 48.1 jit_solution(1475776003781672588)
XLA Ops:
  0.7 3.5 %spectra.1 = bf16[2112,128]{1,0:T(8,128)(2,1)S(1)} custom-call(s32[1,1,8]{2,1,0:T(1,128)} %list_hbm.1, s32[1,1]{1,0:T(1,128)S(6)} %copy.5.count_ref, bf16[2,16,64,1024]{3,2,1,0:T(8,128)(2,1)} %bitcast.7, bf16[128,1024]{1,0:T(8,128)(2,1)} %constant.2.clone.table_hbm), custom_call_target="tpu_custom_call" | custom-call | tf_op jit(solution)/shard_map/spectra/pallas_call | solution.py:75
  4.1 23.0 %all_to_all.10 = bf16[1056,2,128]{2,1,0:T(2,128)(2,1)S(1)} all-to-all(bf16[1056,2,128]{2,1,0:T(2,128)(2,1)S(1)} %bitcast.5), channel_id=1, replica_groups=mesh['shot'=8,'rcv'=4] {'shot','rcv'}, dimensions={0} | all-to-all | bytes 1081344 | tf_op jit(solution)/shard_map/all_to_all | solution.py:219
  27.2 1.0 %products.1 = bf16[32,64,128]{2,1,0:T(8,128)(2,1)S(1)} custom-call(bf16[2112,128]{1,0:T(8,128)(2,1)S(1)} %bitcast.4), custom_call_target="tpu_custom_call" | custom-call | tf_op jit(solution)/shard_map/products/pallas_call | solution.py:159
  28.2 18.5 %all_to_all.11 = bf16[32,64,128]{2,1,0:T(8,128)(2,1)S(1)} all-to-all(bf16[32,64,128]{2,1,0:T(8,128)(2,1)S(1)} %products.1), channel_id=1, replica_groups=mesh['shot'=8,'rcv'=4] {'shot','rcv'}, dimensions={0} | all-to-all | bytes 1048576 | tf_op jit(solution)/shard_map/all_to_all | solution.py:225
  46.6 1.4 %output.1 = f32[64,2,32,64]{3,2,1,0:T(8,128)} custom-call(bf16[64,32,128]{2,1,0:T(8,128)(2,1)S(1)} %bitcast.6), custom_call_target="tpu_custom_call" | custom-call | tf_op jit(solution)/shard_map/output/pallas_call | solution.py:198

commit v7 on v5

--- a/solution.py
+++ b/solution.py
@@ -29,23 +29,23 @@
 def spectra_kernel(destinations, mask_rows, chunks, list_hbm, count_ref, traces_hbm, table_hbm, out_ref, list_ref, traces, table, held, sems):
     half, receivers = traces.shape[1], traces.shape[2]
     rows = out_ref.shape[0] // destinations
-    group = half // chunks
     pitch = PITCH
+    edges = [half * k // 16 for k in (0, 1, 4, 10, 16)]
     copies = [pltpu.make_async_copy(table_hbm, table, sems.at[0])]
     for g in range(chunks):
-        part = pl.ds(g * group, group)
+        part = pl.ds(edges[g], edges[g + 1] - edges[g])
         copies.append(pltpu.make_async_copy(traces_hbm.at[:, part], traces.at[:, part], sems.at[1 + g]))
     copies.append(pltpu.make_async_copy(list_hbm, list_ref, sems.at[1 + chunks]))
     for copy in copies:
         copy.start()
     copies[0].wait()
-    for a in range(half):
-        if a % group == 0:
-            copies[1 + a // group].wait()
-        pair = jnp.concatenate([traces[0, a], traces[1, a]], axis=0)
-        held[a * pitch : a * pitch + 2 * FREQS, :] = lax.dot_general(
-            table[...], pair, (((1,), (1,)), ((), ())), preferred_element_type=jnp.float32
-        )
+    for g in range(chunks):
+        copies[1 + g].wait()
+        for a in range(edges[g], edges[g + 1]):
+            pair = jnp.concatenate([traces[0, a], traces[1, a]], axis=0)
+            held[a * pitch : a * pitch + 2 * FREQS, :] = lax.dot_general(
+                table[...], pair, (((1,), (1,)), ((), ())), preferred_element_type=jnp.float32
+            )
     copies[-1].wait()
     low = lax.broadcasted_iota(jnp.int32, (half, LANES), 1) < receivers
     per = FREQS // destinations

time: 48.5 us -> 48.4 us (level)
  no operation moved by 1% of the time
where the time goes in v7:
time: 48.4 us; the launch traced here: 48.2 us
  blocking collectives  41.8 us (86%)
  Pallas kernels  5.73 us (12%)
  between operations  0.67 us (1%)
    all_to_all x1, blocking collectives, local(): lax.all_to_all(sent.reshape(-1, unit, LANES), axes, 0, 0, tiled=True)  23.3 us
    all_to_all x1, blocking collectives, local(): home = lax.all_to_all(made, axes, 0, 0, tiled=True)  18.5 us
    pallas_call x1, Pallas kernels, spectra(): pl.pallas_call(functools.partial(spectra_kernel, destinations, mask_rows,...  3.34 us
    pallas_call x1, Pallas kernels, output(): pl.pallas_call(functools.partial(output_kernel, chunks), in_specs=[pl.Blo...  1.45 us

profile of v7, /device:TPU:0, one launch (start us, length us, event | category | flops | bytes accessed | tf_op | source)
XLA Modules:
  0.0 48.2 jit_solution(5625890434013053832)
XLA Ops:
  0.7 3.3 %spectra.1 = bf16[2176,128]{1,0:T(8,128)(2,1)S(1)} custom-call(s32[1,1,8]{2,1,0:T(1,128)} %list_hbm.1, s32[1,1]{1,0:T(1,128)S(6)} %copy.5.count_ref, bf16[2,16,64,1024]{3,2,1,0:T(8,128)(2,1)} %bitcast.7, bf16[128,1024]{1,0:T(8,128)(2,1)} %constant.2.clone.table_hbm), custom_call_target="tpu_custom_call" | custom-call | tf_op jit(solution)/shard_map/spectra/pallas_call | solution.py:77
  4.0 23.3 %all_to_all.10 = bf16[544,4,128]{2,1,0:T(4,128)(2,1)S(1)} all-to-all(bf16[544,4,128]{2,1,0:T(4,128)(2,1)S(1)} %bitcast.5), channel_id=1, replica_groups=mesh['shot'=8,'rcv'=4] {'shot','rcv'}, dimensions={0} | all-to-all | bytes 1114112 | tf_op jit(solution)/shard_map/all_to_all | solution.py:210
  27.3 0.9 %products.1 = bf16[32,64,128]{2,1,0:T(8,128)(2,1)S(1)} custom-call(bf16[2176,128]{1,0:T(8,128)(2,1)S(1)} %bitcast.4), custom_call_target="tpu_custom_call" | custom-call | tf_op jit(solution)/shard_map/products/pallas_call | solution.py:150
  28.3 18.5 %all_to_all.11 = bf16[32,64,128]{2,1,0:T(8,128)(2,1)S(1)} all-to-all(bf16[32,64,128]{2,1,0:T(8,128)(2,1)S(1)} %products.1), channel_id=1, replica_groups=mesh['shot'=8,'rcv'=4] {'shot','rcv'}, dimensions={0} | all-to-all | bytes 1048576 | tf_op jit(solution)/shard_map/all_to_all | solution.py:216
  46.8 1.4 %output.1 = f32[64,2,32,64]{3,2,1,0:T(8,128)} custom-call(bf16[64,32,128]{2,1,0:T(8,128)(2,1)S(1)} %bitcast.6), custom_call_target="tpu_custom_call" | custom-call | tf_op jit(solution)/shard_map/output/pallas_call | solution.py:189

commit v8 on v5

--- a/solution.py
+++ b/solution.py
@@ -172,9 +172,10 @@
     copies = []
     for g in range(chunks):
         part = slice(g * step, (g + 1) * step)
-        block = in_ref[part].astype(jnp.float32)
-        held[part, 0] = block[:, :, :receivers]
-        held[part, 1] = block[:, :, receivers:]
+        block = in_ref[part]
+        turned = pltpu.roll(block.reshape(-1, LANES), receivers, 1).reshape(block.shape)
+        held[part, 0] = block[:, :, :receivers].astype(jnp.float32)
+        held[part, 1] = turned[:, :, :receivers].astype(jnp.float32)
         copy = pltpu.make_async_copy(held.at[part], out_ref.at[part], sems.at[g])
         copy.start()
         copies.append(copy)

time: 48.5 us -> 48.5 us (level)
  no operation moved by 1% of the time
where the time goes in v8:
time: 48.5 us; the launch traced here: 48.3 us
  blocking collectives  41.8 us (86%)
  Pallas kernels  5.83 us (12%)
  between operations  0.67 us (1%)
    all_to_all x1, blocking collectives, local(): lax.all_to_all(sent.reshape(-1, unit, LANES), axes, 0, 0, tiled=True)  23.3 us
    all_to_all x1, blocking collectives, local(): home = lax.all_to_all(made, axes, 0, 0, tiled=True)  18.5 us
    pallas_call x1, Pallas kernels, spectra(): pl.pallas_call(functools.partial(spectra_kernel, destinations, mask_rows,...  3.44 us
    pallas_call x1, Pallas kernels, output(): pl.pallas_call(functools.partial(output_kernel, chunks), in_specs=[pl.Blo...  1.45 us

profile of v8, /device:TPU:0, one launch (start us, length us, event | category | flops | bytes accessed | tf_op | source)
XLA Modules:
  0.0 48.3 jit_solution(15052405555755500708)
XLA Ops:
  0.7 3.4 %spectra.1 = bf16[2176,128]{1,0:T(8,128)(2,1)S(1)} custom-call(s32[1,1,8]{2,1,0:T(1,128)} %list_hbm.1, s32[1,1]{1,0:T(1,128)S(6)} %copy.5.count_ref, bf16[2,16,64,1024]{3,2,1,0:T(8,128)(2,1)} %bitcast.7, bf16[128,1024]{1,0:T(8,128)(2,1)} %constant.2.clone.table_hbm), custom_call_target="tpu_custom_call" | custom-call | tf_op jit(solution)/shard_map/spectra/pallas_call | solution.py:77
  4.1 23.3 %all_to_all.10 = bf16[544,4,128]{2,1,0:T(4,128)(2,1)S(1)} all-to-all(bf16[544,4,128]{2,1,0:T(4,128)(2,1)S(1)} %bitcast.5), channel_id=1, replica_groups=mesh['shot'=8,'rcv'=4] {'shot','rcv'}, dimensions={0} | all-to-all | bytes 1114112 | tf_op jit(solution)/shard_map/all_to_all | solution.py:211
  27.4 0.9 %products.1 = bf16[32,64,128]{2,1,0:T(8,128)(2,1)S(1)} custom-call(bf16[2176,128]{1,0:T(8,128)(2,1)S(1)} %bitcast.4), custom_call_target="tpu_custom_call" | custom-call | tf_op jit(solution)/shard_map/products/pallas_call | solution.py:150
  28.4 18.5 %all_to_all.11 = bf16[32,64,128]{2,1,0:T(8,128)(2,1)S(1)} all-to-all(bf16[32,64,128]{2,1,0:T(8,128)(2,1)S(1)} %products.1), channel_id=1, replica_groups=mesh['shot'=8,'rcv'=4] {'shot','rcv'}, dimensions={0} | all-to-all | bytes 1048576 | tf_op jit(solution)/shard_map/all_to_all | solution.py:217
  46.9 1.4 %output.1 = f32[64,2,32,64]{3,2,1,0:T(8,128)} custom-call(bf16[64,32,128]{2,1,0:T(8,128)(2,1)S(1)} %bitcast.6), custom_call_target="tpu_custom_call" | custom-call | tf_op jit(solution)/shard_map/output/pallas_call | solution.py:190

commit v9 on v7

--- a/solution.py
+++ b/solution.py
@@ -172,9 +172,10 @@
     copies = []
     for g in range(chunks):
         part = slice(g * step, (g + 1) * step)
-        block = in_ref[part].astype(jnp.float32)
-        held[part, 0] = block[:, :, :receivers]
-        held[part, 1] = block[:, :, receivers:]
+        block = in_ref[part]
+        turned = pltpu.roll(block.reshape(-1, LANES), receivers, 1).reshape(block.shape)
+        held[part, 0] = block[:, :, :receivers].astype(jnp.float32)
+        held[part, 1] = turned[:, :, :receivers].astype(jnp.float32)
         copy = pltpu.make_async_copy(held.at[part], out_ref.at[part], sems.at[g])
         copy.start()
         copies.append(copy)

time: 48.4 us -> 48.4 us (level)
  no operation moved by 1% of the time
where the time goes in v9:
time: 48.4 us; the launch traced here: 48.2 us
  blocking collectives  41.8 us (86%)
  Pallas kernels  5.73 us (12%)
  between operations  0.67 us (1%)
    all_to_all x1, blocking collectives, local(): lax.all_to_all(sent.reshape(-1, unit, LANES), axes, 0, 0, tiled=True)  23.3 us
    all_to_all x1, blocking collectives, local(): home = lax.all_to_all(made, axes, 0, 0, tiled=True)  18.5 us
    pallas_call x1, Pallas kernels, spectra(): pl.pallas_call(functools.partial(spectra_kernel, destinations, mask_rows,...  3.34 us
    pallas_call x1, Pallas kernels, output(): pl.pallas_call(functools.partial(output_kernel, chunks), in_specs=[pl.Blo...  1.45 us

profile of v9, /device:TPU:0, one launch (start us, length us, event | category | flops | bytes accessed | tf_op | source)
XLA Modules:
  0.0 48.2 jit_solution(4836591978019441554)
XLA Ops:
  0.7 3.3 %spectra.1 = bf16[2176,128]{1,0:T(8,128)(2,1)S(1)} custom-call(s32[1,1,8]{2,1,0:T(1,128)} %list_hbm.1, s32[1,1]{1,0:T(1,128)S(6)} %copy.5.count_ref, bf16[2,16,64,1024]{3,2,1,0:T(8,128)(2,1)} %bitcast.7, bf16[128,1024]{1,0:T(8,128)(2,1)} %constant.2.clone.table_hbm), custom_call_target="tpu_custom_call" | custom-call | tf_op jit(solution)/shard_map/spectra/pallas_call | solution.py:77
  4.0 23.3 %all_to_all.10 = bf16[544,4,128]{2,1,0:T(4,128)(2,1)S(1)} all-to-all(bf16[544,4,128]{2,1,0:T(4,128)(2,1)S(1)} %bitcast.5), channel_id=1, replica_groups=mesh['shot'=8,'rcv'=4] {'shot','rcv'}, dimensions={0} | all-to-all | bytes 1114112 | tf_op jit(solution)/shard_map/all_to_all | solution.py:211
  27.3 0.9 %products.1 = bf16[32,64,128]{2,1,0:T(8,128)(2,1)S(1)} custom-call(bf16[2176,128]{1,0:T(8,128)(2,1)S(1)} %bitcast.4), custom_call_target="tpu_custom_call" | custom-call | tf_op jit(solution)/shard_map/products/pallas_call | solution.py:150
  28.3 18.5 %all_to_all.11 = bf16[32,64,128]{2,1,0:T(8,128)(2,1)S(1)} all-to-all(bf16[32,64,128]{2,1,0:T(8,128)(2,1)S(1)} %products.1), channel_id=1, replica_groups=mesh['shot'=8,'rcv'=4] {'shot','rcv'}, dimensions={0} | all-to-all | bytes 1048576 | tf_op jit(solution)/shard_map/all_to_all | solution.py:217
  46.8 1.4 %output.1 = f32[64,2,32,64]{3,2,1,0:T(8,128)} custom-call(bf16[64,32,128]{2,1,0:T(8,128)(2,1)S(1)} %bitcast.6), custom_call_target="tpu_custom_call" | custom-call | tf_op jit(solution)/shard_map/output/pallas_call | solution.py:190
